TPU v7x, 32 devices: a whole 2x2x4 slice. The times are simulated.
32 devices in a mesh: row: 4 (over z), col: 8 (over y, x, core).
Axes of the slice: x: 2, y: 2, z: 4, core: 2. Of those that a mesh axis runs over, the one named last changes fastest.
Arguments:
- state_start: bfloat16 [512, 2048], P('row', 'col'), may hold values from -360 to 360
- actions: int32 [512, 2], P('row'), may hold values from 0 to 17
- targets: bfloat16 [2, 512, 2048], P(None, 'row'), may hold values from -504 to 504
- w_in: bfloat16 [2048, 4096], P('row', 'col'), may hold values from -0.125 to 0.125
- w_out: bfloat16 [4096, 2048], P('col', 'row'), may hold values from -0.09375 to 0.09375
- action_embed: bfloat16 [18, 4096], P(None, 'col'), may hold values from -6 to 6
Outputs:
- grad_w_in: float32 [2048, 4096], P('row', 'col')
- grad_w_out: float32 [4096, 2048], P('col', 'row')
All inputs are finite; a program needn't handle non-finite values.
Results may differ from a plain program's by a relative error of at most 0.035.
Values may be sent and summed in bfloat16 or wider, within the bound.
A program may use at most 64 MiB of HBM per device.

v0:
```python
import functools

import jax
import jax.numpy as jnp
from jax import lax
from jax.experimental import pallas as pl
from jax.experimental.pallas import tpu as pltpu
from jax.sharding import PartitionSpec as P

EPS = 1e-06
LOSS_SCALE = 128.0
MESH = pl.DeviceIdType.MESH
F32 = jnp.float32
BF16 = jnp.bfloat16


def silu_grad(pre_act):
    gate_val = jax.nn.sigmoid(pre_act)
    return gate_val * (1.0 + pre_act * (1.0 - gate_val))


def cosine_from(state_f, target_f, self_dot, cross_dot, target_dot):
    inv_state = lax.rsqrt(self_dot + EPS)
    inv_target = lax.rsqrt(target_dot + EPS)
    cosine = cross_dot * inv_state * inv_target
    return -LOSS_SCALE * (
        target_f * inv_state * inv_target - cosine * state_f * inv_state * inv_state
    )


def shared_cosine(state, target):
    state_f = state.astype(jnp.float32)
    target_f = target.astype(jnp.float32)
    self_dot, cross_dot, target_dot = lax.psum(
        (
            jnp.sum(state_f * state_f, axis=-1),
            jnp.sum(state_f * target_f, axis=-1),
            jnp.sum(target_f * target_f, axis=-1),
        ),
        "col",
    )
    return cosine_from(
        state_f, target_f, self_dot[:, None], cross_dot[:, None], target_dot[:, None]
    )


def gathered(state_start, actions, targets, w_in, w_out, action_embed):
    unroll_steps = targets.shape[0]
    col_width = state_start.shape[1]
    w_in_panel = lax.all_gather(w_in, "row", axis=0, tiled=True)
    w_out_panel = lax.all_gather(w_out, "row", axis=1, tiled=True)
    col_start = lax.axis_index("col") * col_width
    action_ids = jnp.arange(action_embed.shape[0], dtype=jnp.int32)
    contract_last = (((1,), (1,)), ((), ()))
    current = state_start
    full_states = []
    pre_list = []
    hidden_list = []
    cos_terms = []
    for unroll in range(unroll_steps):
        full_rows = lax.all_gather(current, "col", axis=1, tiled=True)
        onehot = (actions[:, unroll][:, None] == action_ids[None, :]).astype(jnp.bfloat16)
        pre_act = jnp.dot(full_rows, w_in_panel, preferred_element_type=jnp.float32) + jnp.dot(
            onehot, action_embed, preferred_element_type=jnp.float32
        )
        hidden = jax.nn.silu(pre_act).astype(jnp.bfloat16)
        partial_value = jnp.dot(hidden, w_out_panel, preferred_element_type=jnp.float32)
        target = targets[unroll]
        branch = lax.psum_scatter(
            partial_value.astype(jnp.bfloat16), "col", scatter_dimension=1, tiled=True
        ).astype(jnp.float32)
        current = (current.astype(jnp.float32) + branch).astype(jnp.bfloat16)
        target_slice = lax.dynamic_slice_in_dim(target, col_start, col_width, 1)
        cos_terms.append(shared_cosine(current, target_slice))
        full_states.append(full_rows)
        pre_list.append(pre_act)
        hidden_list.append(hidden)
    state_grad = cos_terms[unroll_steps - 1].astype(jnp.bfloat16)
    grad_list = [None] * unroll_steps
    hid_grads = [None] * unroll_steps
    for unroll in reversed(range(unroll_steps)):
        grad_rows = lax.all_gather(state_grad, "col", axis=1, tiled=True)
        back = lax.dot_general(
            grad_rows, w_out_panel, contract_last, preferred_element_type=jnp.float32
        )
        hid_grad = (back * silu_grad(pre_list[unroll])).astype(jnp.bfloat16)
        grad_list[unroll] = grad_rows
        hid_grads[unroll] = hid_grad
        if unroll > 0:
            input_part = lax.dot_general(
                hid_grad, w_in_panel, contract_last, preferred_element_type=jnp.float32
            )
            summed = lax.psum_scatter(
                input_part.astype(jnp.bfloat16), "col", scatter_dimension=1, tiled=True
            ).astype(jnp.float32)
            state_grad = (state_grad.astype(jnp.float32) + summed + cos_terms[unroll - 1]).astype(
                jnp.bfloat16
            )
    grad_stack = jnp.stack(grad_list)
    hidden_stack = jnp.stack(hidden_list)
    state_stack = jnp.stack(full_states)
    hid_stack = jnp.stack(hid_grads)
    grad_feature_blocks = lax.all_to_all(grad_stack, "row", split_axis=2, concat_axis=1, tiled=True)
    hidden_all = lax.all_gather(hidden_stack, "row", axis=1, tiled=True)
    grad_w_out = jnp.einsum(
        "kbf,kbd->fd", hidden_all, grad_feature_blocks, preferred_element_type=jnp.float32
    )
    state_feature_blocks = lax.all_to_all(
        state_stack, "row", split_axis=2, concat_axis=1, tiled=True
    )
    hid_all = lax.all_gather(hid_stack, "row", axis=1, tiled=True)
    grad_w_in = jnp.einsum(
        "kbd,kbf->df", state_feature_blocks, hid_all, preferred_element_type=jnp.float32
    )
    return (grad_w_in, grad_w_out)


def sem_plan(nr, nc):
    at = {}
    total = 0
    for name, count in (
        [("start", nr), ("targets", nr)]
        + [(f"cag{i}", nr * nc) for i in range(4)]
        + [(f"zrs{i}", 2 * nr) for i in range(4)]
        + [(f"zag{i}", 2 * nr) for i in range(4)]
        + [(f"crs{i}", nr * nc) for i in range(3)]
        + [(f"dot{i}", 2 * nr) for i in range(2)]
    ):
        at[name] = total
        total += count
    return at, total


def sends_in_all(nr, nc):
    per = nc // 2
    return per + (nr - 1) * (1 + 8 + 8 + 4) + 4 * nr * (nc - 1) + 3 * 2 * nr * per


def kernel(
    nr, nc, st, act, tg, wi, wo, emb, gwi, gwo,
    s0p, tgp, sfull, hfull, efull, gfull, psend, zr, ysend, cr, own, pre, dsend, dz,
    send_sem, recv_sem,
):
    r, c = lax.axis_index("row"), lax.axis_index("col")
    piece, df = sfull.shape[3], sfull.shape[4]
    per, pair = nc // 2, nr // 2
    rows = per * piece
    home, half = lax.div(c, 2), lax.rem(c, 2)
    place, first = lax.div(c, 2), half * pair
    side = lax.div(r, pair)
    at, _ = sem_plan(nr, nc)
    started = []
    unused = iter(range(10000))

    def zpeer(o):
        return lax.rem(r + o, nr)

    def cpeer(o):
        return lax.rem(c + o, nc)

    def copy(src, dst, sem, slot, dev):
        return pltpu.make_async_remote_copy(
            src_ref=src, dst_ref=dst, send_sem=send_sem.at[sem], recv_sem=recv_sem.at[slot],
            device_id=dev, device_id_type=MESH,
        )

    def send(src, dst, slot, dev, when=None):
        sem = next(unused)
        started.append((src, dst, sem, slot, dev, when))
        if when is None:
            copy(src, dst, sem, slot, dev).start()
        else:
            pl.when(when)(lambda: copy(src, dst, sem, slot, dev).start())

    def arrived(dst, slot, dev, when=None):
        if when is None:
            copy(dst, dst, 0, slot, dev).wait_recv()
        else:
            pl.when(when)(lambda: copy(dst, dst, 0, slot, dev).wait_recv())

    barrier = pltpu.get_barrier_semaphore()
    for o in range(1, nr):
        pl.semaphore_signal(barrier, inc=1, device_id=(zpeer(o), c), device_id_type=MESH)
    for o in range(1, nc):
        pl.semaphore_signal(barrier, inc=1, device_id=(r, cpeer(o)), device_id_type=MESH)
    for hf in range(2):
        for i in range(pair):

            @pl.when((2 * r + hf != c) | (first + i != r))
            def _():
                pl.semaphore_signal(
                    barrier, inc=1, device_id=(first + i, 2 * r + hf), device_id_type=MESH
                )

    away = (home != r) | (half != side)
    pl.semaphore_wait(barrier, (nr - 1) + (nc - 1) + (per - 1) + jnp.where(away, 1, 0))

    mine = half * pair + lax.rem(r, pair)
    for o in range(per):
        p = lax.rem(place + o, per)
        send(
            st.at[:, p], s0p.at[half, lax.rem(r, pair)], at["start"] + mine,
            (home, 2 * p + side), away if o == 0 else None,
        )

    @pl.when(jnp.logical_not(away))
    def _():
        s0p[half, lax.rem(r, pair)] = st[:, place]

    for hf in range(2):
        for i in range(pair):
            arrived(
                s0p.at[hf, i], at["start"] + hf * pair + i, (first + i, 2 * r + hf),
                (2 * r + hf != c) | (first + i != r),
            )

    order = [zpeer(o) for o in range(1, nr)] + [r]
    back_order = [r] + [zpeer(o) for o in range(1, nr)]

    def spread(full, name, i, k):
        b, q = first + i, per * k + place
        for o in range(1, nc):
            send(full.at[b, q], full.at[b, q], at[name] + b * nc + q, (r, cpeer(o)))

    def collect(full, name, b, k):
        for o in range(per):
            p = lax.rem(place + o, per)
            q = per * k + p
            arrived(
                full.at[b, q], at[name] + b * nc + q, (r, 2 * p + lax.div(b, pair)),
                lax.div(b, pair) != half if o == 0 else None,
            )

    def mm(a, b, dims):
        return lax.dot_general(a, b, (dims, ((), ())), preferred_element_type=F32)

    def block(full, b, k):
        return full[b, per * k:per * (k + 1)].reshape(rows, df)

    def reduce_rows(full, name, weight, dims, phase, k):
        for o in range(1, nr):
            b = zpeer(o)
            collect(full, name, b, k)
            psend[phase, b, k] = mm(block(full, b, k), weight[...], dims).astype(BF16)
            send(
                psend.at[phase, b, k], zr.at[phase, r, k],
                at[f"zrs{phase}"] + 2 * r + k, (b, c),
            )
        collect(full, name, r, k)
        return mm(block(full, r, k), weight[...], dims)

    def reduced(total, phase, k):
        for o in range(nr - 1, 0, -1):
            b = zpeer(o)
            arrived(zr.at[phase, b, k], at[f"zrs{phase}"] + 2 * b + k, (b, c))
            total = total + zr[phase, b, k].astype(F32)
        return total

    def share_rows(full, phase, k):
        for o in range(1, nr):
            send(full.at[r, k], full.at[r, k], at[f"zag{phase}"] + 2 * r + k, (zpeer(o), c))

    def shared(full, phase, b, k):
        arrived(full.at[b, k], at[f"zag{phase}"] + 2 * b + k, (b, c))

    def group_terms(full, zphase, weight, dims, phase, k):
        for b in [r] + [zpeer(o) for o in range(nr - 1, 0, -1)]:
            if b is not r:
                shared(full, zphase, b, k)
            term = mm(full[b, k], weight[...], dims).astype(BF16)
            ysend[phase, b, per * k:per * (k + 1)] = term.reshape(per, piece, df)
            slot = at[f"crs{phase}"] + (lax.rem(b, pair) * 2 + k) * nc + c
            for o in range(per - 1, -1, -1):
                p = lax.rem(place + o, per)
                send(
                    ysend.at[phase, b, per * k + p], cr.at[phase, lax.rem(b, pair), k, c], slot,
                    (r, 2 * p + lax.div(b, pair)),
                    lax.div(b, pair) != half if o == 0 else None,
                )

    def group_total(phase, i, k):
        total = ysend[phase, first + i, per * k + place].astype(F32)
        for o in range(1, nc):
            j = cpeer(o)
            arrived(cr.at[phase, i, k, j], at[f"crs{phase}"] + (i * 2 + k) * nc + j, (r, j))
            total = total + cr[phase, i, k, j].astype(F32)
        return total

    lane = lax.broadcasted_iota(jnp.int32, (piece, 128), 1)

    def dots(u, k):
        for i in range(pair):
            s = own[u, i, k].astype(F32)
            t = tgp[i, u, k].astype(F32)
            ss = jnp.sum(s * s, axis=-1, keepdims=True)
            sc = jnp.sum(s * t, axis=-1, keepdims=True)
            tt = jnp.sum(t * t, axis=-1, keepdims=True)
            both = jnp.where(lane == 0, ss, jnp.where(lane == 1, sc, tt))
            dsend[u, k, i] = both
            dz[u, k, r, i] = both
        for o in range(1, nr):
            send(dsend.at[u, k], dz.at[u, k, r], at[f"dot{u}"] + 2 * r + k, (zpeer(o), c))

    def dots_in(u, k):
        for o in range(1, nr):
            b = zpeer(o)
            arrived(dz.at[u, k, b], at[f"dot{u}"] + 2 * b + k, (b, c))

    def cosine(u, i, k):
        total = dz[u, k, 0, i]
        for z in range(1, nr):
            total = total + dz[u, k, z, i]
        return cosine_from(
            own[u, i, k].astype(F32), tgp[i, u, k].astype(F32),
            total[:, 0:1], total[:, 1:2], total[:, 2:3],
        )

    ids = lax.broadcasted_iota(jnp.int32, (rows, emb.shape[0]), 1)
    plain, flipped, over_rows = ((1,), (0,)), ((1,), (1,)), ((0,), (0,))

    def into_hidden(u, k):
        total = reduce_rows(sfull.at[u], f"cag{u}", wi, plain, u, k)
        onehot = (act[rows * k:rows * (k + 1), u:u + 1] == ids).astype(F32).astype(BF16)
        pre[u, k] = total + mm(onehot, emb[...], plain)

    def hidden(u, k):
        total = reduced(pre[u, k], u, k)
        pre[u, k] = total
        hfull[u, r, k] = (total * jax.nn.sigmoid(total)).astype(BF16)
        share_rows(hfull.at[u], u, k)

    def next_state(u, k):
        for i in range(pair):
            old = sfull[u, first + i, per * k + place].astype(F32)
            new = (old + group_total(u, i, k)).astype(BF16)
            own[u, i, k] = new
            if u == 0:
                sfull[1, first + i, per * k + place] = new
                spread(sfull.at[1], "cag1", i, k)

    def last_grad(k):
        dots_in(1, k)
        for i in range(pair):
            gfull[1, first + i, per * k + place] = cosine(1, i, k).astype(BF16)
            spread(gfull.at[1], "cag2", i, k)

    def into_back(u, k):
        back[k] = reduce_rows(gfull.at[u], f"cag{3 - u}", wo, flipped, 3 - u, k)

    def hidden_grad(u, k):
        total = reduced(back[k], 3 - u, k)
        efull[u, r, k] = (total * silu_grad(pre[u, k])).astype(BF16)
        share_rows(efull.at[u], 3 - u, k)

    def first_grad(k):
        dots_in(0, k)
        for i in range(pair):
            b, q = first + i, per * k + place
            summed = gfull[1, b, q].astype(F32) + group_total(2, i, k) + cosine(0, i, k)
            gfull[0, b, q] = summed.astype(BF16)
            spread(gfull.at[0], "cag3", i, k)

    back = [None, None]
    for k in range(2):
        for i in range(pair):
            sfull[0, first + i, per * k + place] = jnp.concatenate(
                [s0p[0, i, k], s0p[1, i, k]], axis=-1
            )
            spread(sfull.at[0], "cag0", i, k)
    into_hidden(0, 0)
    into_hidden(0, 1)

    for o in range(1, nr):
        b = zpeer(o)
        send(
            tg.at[:, :, place, :, pl.ds(pl.multiple_of(b * df, df), df)],
            tgp.at[lax.rem(r, pair)], at["targets"] + lax.rem(r, pair), (b, c), side == half,
        )

    @pl.when(side == half)
    def _():
        tgp[lax.rem(r, pair)] = tg[:, :, place, :, pl.ds(pl.multiple_of(r * df, df), df)]

    hidden(0, 0)
    hidden(0, 1)
    group_terms(hfull.at[0], 0, wo, plain, 0, 0)
    next_state(0, 0)
    group_terms(hfull.at[0], 0, wo, plain, 0, 1)
    into_hidden(1, 0)
    next_state(0, 1)
    into_hidden(1, 1)
    for i in range(pair):
        arrived(tgp.at[i], at["targets"] + i, (first + i, c), first + i != r)
    hidden(1, 0)
    hidden(1, 1)
    dots(0, 0)
    dots(0, 1)
    group_terms(hfull.at[1], 1, wo, plain, 1, 0)
    next_state(1, 0)
    dots(1, 0)
    group_terms(hfull.at[1], 1, wo, plain, 1, 1)
    last_grad(0)
    next_state(1, 1)
    dots(1, 1)
    into_back(1, 0)
    last_grad(1)
    into_back(1, 1)
    hidden_grad(1, 0)
    hidden_grad(1, 1)
    group_terms(efull.at[1], 2, wi, flipped, 2, 0)
    first_grad(0)
    group_terms(efull.at[1], 2, wi, flipped, 2, 1)
    into_back(0, 0)
    first_grad(1)
    into_back(0, 1)

    def tall(x):
        return x.reshape(nr * nc * piece, x.shape[-1])

    hidden_grad(0, 0)
    hidden_grad(0, 1)
    gwo[...] = mm(tall(hfull[1]), tall(gfull[1]), over_rows)
    gwi[...] = mm(tall(sfull[1]), tall(efull[1]), over_rows)
    gwo[...] += mm(tall(hfull[0]), tall(gfull[0]), over_rows)
    for k in range(2):
        for b in order[:-1]:
            shared(efull.at[0], 3, b, k)
    gwi[...] += mm(tall(sfull[0]), tall(efull[0]), over_rows)

    for src, dst, sem, slot, dev, when in started:
        if when is None:
            copy(src, dst, sem, slot, dev).wait_send()
        else:
            pl.when(when)(lambda: copy(src, dst, sem, slot, dev).wait_send())


def stationary(nr, nc, state_start, actions, targets, w_in, w_out, action_embed):
    rb, sw = state_start.shape
    piece = rb // nc
    per, pair, rows = nc // 2, nr // 2, rb // 2
    df, fc = w_in.shape
    vm = pl.BlockSpec(memory_space=pltpu.VMEM)
    _, receives = sem_plan(nr, nc)
    return pl.pallas_call(
        functools.partial(kernel, nr, nc),
        out_shape=(
            jax.ShapeDtypeStruct((df, fc), F32),
            jax.ShapeDtypeStruct((fc, df), F32),
        ),
        in_specs=[vm] * 6,
        out_specs=(vm, vm),
        scratch_shapes=[
            pltpu.VMEM((2, pair, 2, piece, sw), BF16),
            pltpu.VMEM((pair, 2, 2, piece, df), BF16),
            pltpu.VMEM((2, nr, nc, piece, df), BF16),
            pltpu.VMEM((2, nr, 2, rows, fc), BF16),
            pltpu.VMEM((2, nr, 2, rows, fc), BF16),
            pltpu.VMEM((2, nr, nc, piece, df), BF16),
            pltpu.VMEM((4, nr, 2, rows, fc), BF16),
            pltpu.VMEM((4, nr, 2, rows, fc), BF16),
            pltpu.VMEM((3, nr, nc, piece, df), BF16),
            pltpu.VMEM((3, pair, 2, nc, piece, df), BF16),
            pltpu.VMEM((2, pair, 2, piece, df), BF16),
            pltpu.VMEM((2, 2, rows, fc), F32),
            pltpu.VMEM((2, 2, pair, piece, 128), F32),
            pltpu.VMEM((2, 2, nr, pair, piece, 128), F32),
            pltpu.SemaphoreType.DMA((sends_in_all(nr, nc),)),
            pltpu.SemaphoreType.DMA((receives,)),
        ],
        compiler_params=pltpu.CompilerParams(
            collective_id=0, has_side_effects=True, vmem_limit_bytes=56 * 1024 * 1024
        ),
    )(
        state_start.reshape(2, per, piece, sw),
        actions,
        targets.reshape(targets.shape[0], 2, per, piece, targets.shape[2]),
        w_in,
        w_out,
        action_embed,
    )


def solution(mesh):
    nr, nc = mesh.shape["row"], mesh.shape["col"]

    def on_device(state_start, actions, targets, w_in, w_out, action_embed):
        rb, sw = state_start.shape
        fits = (
            targets.shape[0] == 2
            and nc == 2 * nr
            and nr % 2 == 0
            and rb % (16 * nc) == 0
            and sw % 128 == 0
            and w_in.shape[0] % 128 == 0
            and w_in.shape[1] % 128 == 0
        )
        args = (state_start, actions, targets, w_in, w_out, action_embed)
        if fits:
            return stationary(nr, nc, *args)
        return gathered(*args)

    in_specs = (
        P("row", "col"),
        P("row", None),
        P(None, "row", None),
        P("row", "col"),
        P("col", "row"),
        P(None, "col"),
    )
    out_specs = (P("row", "col"), P("col", "row"))
    return jax.shard_map(
        on_device, mesh=mesh, in_specs=in_specs, out_specs=out_specs, check_vma=False
    )
```

profile of v0, /device:TPU:0, one launch (start us, length us, event | category | flops | bytes accessed | tf_op | source)
XLA Modules:
  0.0 144.8 jit_solution(16708161500940400801)
XLA Ops:
  0.6 0.0 copy-start.1
  0.6 0.7 copy-done.1
  1.3 0.7 copy.8.act
  2.0 139.4 %shard_map.77 = (f32[512,512]{1,0:T(8,128)}, f32[512,512]{1,0:T(8,128)}) custom-call(bf16[2,4,16,256]{3,2,1,0:T(8,128)(2,1)} %bitcast.3, s32[128,2]{1,0:T(8,128)} %copy.8.act, bf16[2,2,4,16,2048]{4,3,2,1,0:T(8,128)(2,1)} %bitcast.2, bf16[512,512]{1,0:T(8,128)(2,1)} %wi.1, bf16[512,512]{1,0:T(8,128)(2,1)} %wo.1, bf16[18,512]{1,0:T(8,128)(2,1)} %emb.1), custom_call_target="tpu_custom_call" | custom-call | tf_op jit(solution)/shard_map/pallas_call | solution.py:444
  141.5 0.0 copy-start
  141.5 2.4 %copy.11 = f32[512,512]{1,0:T(8,128)} copy(f32[512,512]{1,0:T(8,128)} %get-tuple-element.4) | data formatting | bytes 2097152
  143.8 0.0 copy-done
  143.8 1.0 copy.12
Async XLA Ops:
  0.6 0.7 copy-start.1
  141.5 2.4 %copy-start = (f32[512,512]{1,0:T(8,128)S(1)}, f32[512,512]{1,0:T(8,128)}, u32[]{:S(2)}) copy-start(f32[512,512]{1,0:T(8,128)} %get-tuple-element.5) | copy-start | bytes 3145732
where the time goes:
time: 147 us; the launch traced here: 145 us
  Pallas kernels  139 us (95%)
  local copies, waits for them, and re-layouts  4.74 us (3%)
    pallas_call x1, Pallas kernels, stationary(): pl.pallas_call(functools.partial(kernel, nr, nc), out_shape=(jax.ShapeDty...  139 us
    unnamed x7, local copies, waits for them, and re-layouts  4.74 us

commit v1 on v0

v1 whole, which is shorter than its diff:
```python
import functools

import jax
import jax.numpy as jnp
from jax import lax
from jax.experimental import pallas as pl
from jax.experimental.pallas import tpu as pltpu
from jax.sharding import PartitionSpec as P

EPS = 1e-06
LOSS_SCALE = 128.0
MESH = pl.DeviceIdType.MESH
F32 = jnp.float32
BF16 = jnp.bfloat16


def silu_grad(pre_act):
    gate_val = jax.nn.sigmoid(pre_act)
    return gate_val * (1.0 + pre_act * (1.0 - gate_val))


def cosine_from(state_f, target_f, self_dot, cross_dot, target_dot):
    inv_state = lax.rsqrt(self_dot + EPS)
    inv_target = lax.rsqrt(target_dot + EPS)
    cosine = cross_dot * inv_state * inv_target
    return -LOSS_SCALE * (
        target_f * inv_state * inv_target - cosine * state_f * inv_state * inv_state
    )


def shared_cosine(state, target):
    state_f = state.astype(jnp.float32)
    target_f = target.astype(jnp.float32)
    self_dot, cross_dot, target_dot = lax.psum(
        (
            jnp.sum(state_f * state_f, axis=-1),
            jnp.sum(state_f * target_f, axis=-1),
            jnp.sum(target_f * target_f, axis=-1),
        ),
        "col",
    )
    return cosine_from(
        state_f, target_f, self_dot[:, None], cross_dot[:, None], target_dot[:, None]
    )


def gathered(state_start, actions, targets, w_in, w_out, action_embed):
    unroll_steps = targets.shape[0]
    col_width = state_start.shape[1]
    w_in_panel = lax.all_gather(w_in, "row", axis=0, tiled=True)
    w_out_panel = lax.all_gather(w_out, "row", axis=1, tiled=True)
    col_start = lax.axis_index("col") * col_width
    action_ids = jnp.arange(action_embed.shape[0], dtype=jnp.int32)
    contract_last = (((1,), (1,)), ((), ()))
    current = state_start
    full_states = []
    pre_list = []
    hidden_list = []
    cos_terms = []
    for unroll in range(unroll_steps):
        full_rows = lax.all_gather(current, "col", axis=1, tiled=True)
        onehot = (actions[:, unroll][:, None] == action_ids[None, :]).astype(jnp.bfloat16)
        pre_act = jnp.dot(full_rows, w_in_panel, preferred_element_type=jnp.float32) + jnp.dot(
            onehot, action_embed, preferred_element_type=jnp.float32
        )
        hidden = jax.nn.silu(pre_act).astype(jnp.bfloat16)
        partial_value = jnp.dot(hidden, w_out_panel, preferred_element_type=jnp.float32)
        target = targets[unroll]
        branch = lax.psum_scatter(
            partial_value.astype(jnp.bfloat16), "col", scatter_dimension=1, tiled=True
        ).astype(jnp.float32)
        current = (current.astype(jnp.float32) + branch).astype(jnp.bfloat16)
        target_slice = lax.dynamic_slice_in_dim(target, col_start, col_width, 1)
        cos_terms.append(shared_cosine(current, target_slice))
        full_states.append(full_rows)
        pre_list.append(pre_act)
        hidden_list.append(hidden)
    state_grad = cos_terms[unroll_steps - 1].astype(jnp.bfloat16)
    grad_list = [None] * unroll_steps
    hid_grads = [None] * unroll_steps
    for unroll in reversed(range(unroll_steps)):
        grad_rows = lax.all_gather(state_grad, "col", axis=1, tiled=True)
        back = lax.dot_general(
            grad_rows, w_out_panel, contract_last, preferred_element_type=jnp.float32
        )
        hid_grad = (back * silu_grad(pre_list[unroll])).astype(jnp.bfloat16)
        grad_list[unroll] = grad_rows
        hid_grads[unroll] = hid_grad
        if unroll > 0:
            input_part = lax.dot_general(
                hid_grad, w_in_panel, contract_last, preferred_element_type=jnp.float32
            )
            summed = lax.psum_scatter(
                input_part.astype(jnp.bfloat16), "col", scatter_dimension=1, tiled=True
            ).astype(jnp.float32)
            state_grad = (state_grad.astype(jnp.float32) + summed + cos_terms[unroll - 1]).astype(
                jnp.bfloat16
            )
    grad_stack = jnp.stack(grad_list)
    hidden_stack = jnp.stack(hidden_list)
    state_stack = jnp.stack(full_states)
    hid_stack = jnp.stack(hid_grads)
    grad_feature_blocks = lax.all_to_all(grad_stack, "row", split_axis=2, concat_axis=1, tiled=True)
    hidden_all = lax.all_gather(hidden_stack, "row", axis=1, tiled=True)
    grad_w_out = jnp.einsum(
        "kbf,kbd->fd", hidden_all, grad_feature_blocks, preferred_element_type=jnp.float32
    )
    state_feature_blocks = lax.all_to_all(
        state_stack, "row", split_axis=2, concat_axis=1, tiled=True
    )
    hid_all = lax.all_gather(hid_stack, "row", axis=1, tiled=True)
    grad_w_in = jnp.einsum(
        "kbd,kbf->df", state_feature_blocks, hid_all, preferred_element_type=jnp.float32
    )
    return (grad_w_in, grad_w_out)


CHUNKS = 4
STAGES = (
    ("into_hidden", 0, 0.0, 1.0),
    ("hidden", 0, 5.5, 2.4),
    ("other_terms", 0, 12.0, 1.0),
    ("next_state", 0, 16.0, 1.0),
    ("into_hidden", 1, 20.0, 1.0),
    ("hidden", 1, 25.5, 2.4),
    ("next_state", 1, 30.5, 2.4),
    ("last_grad", 1, 33.8, 2.4),
    ("into_back", 1, 38.0, 2.4),
    ("hidden_grad", 1, 43.5, 2.4),
    ("first_grad", 0, 48.0, 2.4),
    ("into_back", 0, 52.0, 2.4),
    ("hidden_grad", 0, 57.5, 2.4),
)


def stage_order():
    at = [
        (start + lag * k, i, k)
        for i, (_, _, start, lag) in enumerate(STAGES)
        for k in range(CHUNKS)
    ]
    return [(STAGES[i][0], STAGES[i][1], k) for _, i, k in sorted(at)]


def sem_plan(nc):
    at = {}
    total = 0
    for name, count in (
        [("wi", 1), ("wo", CHUNKS), ("s0x", 1), ("s0", nc), ("tg", 1)]
        + [(f"ag{i}", CHUNKS * nc) for i in range(3)]
        + [(f"z{i}", CHUNKS) for i in range(4)]
        + [(f"rs{i}", CHUNKS * nc) for i in range(3)]
        + [(f"dot{i}", CHUNKS * 4) for i in range(2)]
        + [(f"{n}b{u}", CHUNKS) for n in "hesg" for u in range(2)]
    ):
        at[name] = total
        total += count
    return at, total


def sends_in_all(nc):
    return 3 + CHUNKS + 2 * (nc - 1) + CHUNKS * (6 * (nc - 1) + 3 + 4 + 6 + 8)


def kernel(
    st, act, tg, wi, wo, emb, gwi, gwo,
    wix, wox, s0x, tgp, sf, gf, hf, ef, sb, gb, hb, eb, zs, zr, ys, cr, own, pre, ds, dz,
    send_sem, recv_sem,
):
    r, c = lax.axis_index("row"), lax.axis_index("col")
    nr, nc = 4, 8
    groups, piece, df = sf.shape[3], sf.shape[4], sf.shape[5]
    rows = groups * piece
    per = CHUNKS // 2
    sw = st.shape[3]
    a, b = lax.rem(r, 2), lax.div(r, 2)
    p, q = lax.div(c, 2), lax.rem(c, 2)
    near, far = r + 1 - 2 * a, lax.rem(r + 2, nr)
    twin = c + 1 - 2 * q
    at, _ = sem_plan(nc)
    started = []
    unused = iter(range(10000))

    def cpeer(o):
        return lax.rem(c + o, nc)

    def copy(src, dst, sem, slot, dev):
        return pltpu.make_async_remote_copy(
            src_ref=src, dst_ref=dst, send_sem=send_sem.at[sem], recv_sem=recv_sem.at[slot],
            device_id=dev, device_id_type=MESH,
        )

    def send(src, dst, slot, dev, when=None):
        sem = next(unused)
        started.append((src, dst, sem, slot, dev, when))
        if when is None:
            copy(src, dst, sem, slot, dev).start()
        else:
            pl.when(when)(lambda: copy(src, dst, sem, slot, dev).start())

    def arrived(dst, slot, when=None):
        if when is None:
            copy(dst, dst, 0, slot, (near, c)).wait_recv()
        else:
            pl.when(when)(lambda: copy(dst, dst, 0, slot, (near, c)).wait_recv())

    barrier = pltpu.get_barrier_semaphore()
    greeted = [(r, cpeer(o)) for o in range(1, nc)] + [
        (near, c), (far, c), (far, twin), (far, cpeer(nc // 2))
    ]
    for dev in greeted:
        pl.semaphore_signal(barrier, inc=1, device_id=dev, device_id_type=MESH)
    pl.semaphore_wait(barrier, len(greeted))

    home = lax.div(c, nc // 2) == b
    away = jnp.logical_not(home)
    send(st, s0x, at["s0x"], (far, cpeer(nc // 2)), away)
    send(wi, wix, at["wi"], (near, c))

    def place0(block, col):
        i = jnp.where(lax.div(col, nc // 2) == b, b, 1 - b)
        return sf.at[
            0, pl.ds(i * per, per), lax.rem(lax.div(col, 2), 2), :, :,
            pl.ds(pl.multiple_of(lax.rem(col, 2) * sw, sw), sw),
        ]

    for o in range(1, nc):
        send(st, place0(st, c), at["s0"] + c, (r, cpeer(o)), home)
    arrived(s0x, at["s0x"], away)
    for o in range(1, nc):
        send(s0x, place0(s0x, c), at["s0"] + c, (r, cpeer(o)), away)

    @pl.when(home)
    def _():
        place0(st, c)[...] = st[...]

    @pl.when(away)
    def _():
        place0(s0x, c)[...] = s0x[...]

    def send_wo(j):
        part = pl.ds(j * (wo.shape[0] // CHUNKS), wo.shape[0] // CHUNKS)
        send(wo.at[part], wox.at[part], at["wo"] + j, (near, c))

    send_wo(0)

    def mm(x, y, dims):
        return lax.dot_general(x, y, (dims, ((), ())), preferred_element_type=F32)

    def flat(x):
        return x.reshape(-1, x.shape[-1])

    ids = lax.broadcasted_iota(jnp.int32, (rows, emb.shape[0]), 1)
    plain, flipped, over_rows = ((1,), (0,)), ((1,), (1,)), ((0,), (0,))

    def spread(full, name, k):
        for o in range(1, nc):
            send(full.at[k, q, p], full.at[k, q, p], at[name] + k * nc + c, (r, cpeer(o)))

    def collect(full, name, k):
        for o in range(1, nc):
            j = cpeer(o)
            arrived(full.at[k, lax.rem(j, 2), lax.div(j, 2)], at[name] + k * nc + j)

    def exchange(phase, k, part):
        zs[phase, k] = part.astype(BF16)
        send(zs.at[phase, k], zr.at[phase, k], at[f"z{phase}"] + k, (far, c))

    def exchanged(phase, k):
        arrived(zr.at[phase, k], at[f"z{phase}"] + k)
        return zr[phase, k].astype(F32)

    def to_near(name, u, k, src, dst):
        send(src, dst.at[u, k], at[f"{name}b{u}"] + k, (near, c))

    def from_near(name, dst, u):
        for k in range(CHUNKS):
            arrived(dst.at[u, k], at[f"{name}b{u}"] + k)

    def terms(phase, k, left, weight, dims, which):
        ys[phase, k, which] = mm(left, weight[...], dims).astype(BF16).reshape(groups, piece, df)
        for o in range(groups - 1, -1, -1):
            g = lax.rem(p + o, groups)
            send(
                ys.at[phase, k, which, g], cr.at[phase, k, c], at[f"rs{phase}"] + k * nc + c,
                (r, 2 * g + which), which != q if o == 0 else None,
            )

    def total(phase, k):
        out = ys[phase, k, q, p].astype(F32)
        for o in range(1, nc):
            j = cpeer(o)
            arrived(cr.at[phase, k, j], at[f"rs{phase}"] + k * nc + j)
            out = out + cr[phase, k, j].astype(F32)
        return out

    lane = lax.broadcasted_iota(jnp.int32, (piece, 128), 1)

    def target(u, k):
        return tgp[k // per, u, k % per].astype(F32)

    def dots(u, k):
        s = own[u, k].astype(F32)
        t = target(u, k)
        ss = jnp.sum(s * s, axis=-1, keepdims=True)
        sc = jnp.sum(s * t, axis=-1, keepdims=True)
        tt = jnp.sum(t * t, axis=-1, keepdims=True)
        both = jnp.where(lane == 0, ss, jnp.where(lane == 1, sc, tt))
        me = 2 * b + q
        ds[u, k] = both
        dz[u, k, me] = both
        for dev in ((far, c), (far, twin), (r, twin)):
            send(ds.at[u, k], dz.at[u, k, me], at[f"dot{u}"] + k * 4 + me, dev)

    def dots_in(u, k):
        for o in range(1, 4):
            j = lax.rem(2 * b + q + o, 4)
            arrived(dz.at[u, k, j], at[f"dot{u}"] + k * 4 + j)

    def cosine(u, k):
        both = dz[u, k, 0]
        for j in range(1, 4):
            both = both + dz[u, k, j]
        return cosine_from(
            own[u, k].astype(F32), target(u, k), both[:, 0:1], both[:, 1:2], both[:, 2:3]
        )

    def into_hidden(u, k):
        if u > 0:
            collect(sf.at[u], "ag0", k)
        part = mm(flat(sf[u, k, a]), wi[...], plain)
        if u == 0 and k == 0:
            arrived(wix, at["wi"])
        part = part + mm(flat(sf[u, k, 1 - a]), wix[...], plain)
        act_k = act[rows * (k % per):rows * (k % per) + rows, u:u + 1]
        mine = jnp.where(k // per == b, 0, -emb.shape[0])
        onehot = (act_k + mine == ids).astype(F32).astype(BF16)
        part = part + mm(onehot, emb[...], plain)
        pre[u, k] = part
        exchange(u, k, part)
        if u == 0 and k < CHUNKS - 1:
            send_wo(k + 1)
        to_near("s", u, k, sf.at[u, k, 1 - a], sb)

    def hidden(u, k):
        v = pre[u, k] + exchanged(u, k)
        gate = jax.nn.sigmoid(v)
        hf[u, k] = (v * gate).astype(BF16)
        pre[u, k] = gate * (1.0 + v * (1.0 - gate))
        terms(u, k, hf[u, k], wo, plain, a)
        if u > 0:
            other_terms(u, k)

    def other_terms(u, k):
        if u == 0 and k == 0:
            for j in range(CHUNKS):
                part = pl.ds(j * (wo.shape[0] // CHUNKS), wo.shape[0] // CHUNKS)
                arrived(wox.at[part], at["wo"] + j)
        terms(u, k, hf[u, k], wox, plain, 1 - a)
        to_near("h", u, k, hf.at[u, k], hb)

    def next_state(u, k):
        new = (sf[u, k, q, p].astype(F32) + total(u, k)).astype(BF16)
        own[u, k] = new
        if u == 0:
            sf[1, k, q, p] = new
            spread(sf.at[1], "ag0", k)
        dots(u, k)

    def last_grad(u, k):
        dots_in(u, k)
        gf[1, k, q, p] = cosine(u, k).astype(BF16)
        spread(gf.at[1], "ag1", k)

    def into_back(u, k):
        collect(gf.at[u], f"ag{2 - u}", k)
        part = mm(flat(gf[u, k, a]), wo[...], flipped) + mm(
            flat(gf[u, k, 1 - a]), wox[...], flipped
        )
        back[k] = part
        exchange(3 - u, k, part)
        to_near("g", u, k, gf.at[u, k, 1 - a], gb)

    def hidden_grad(u, k):
        ef[u, k] = ((back[k] + exchanged(3 - u, k)) * pre[u, k]).astype(BF16)
        if u > 0:
            terms(2, k, ef[u, k], wi, flipped, a)
            terms(2, k, ef[u, k], wix, flipped, 1 - a)
        to_near("e", u, k, ef.at[u, k], eb)

    def first_grad(u, k):
        if k == 0:
            for j in range(CHUNKS):
                dots_in(0, j)
        summed = gf[1, k, q, p].astype(F32) + total(2, k) + cosine(0, k)
        gf[0, k, q, p] = summed.astype(BF16)
        spread(gf.at[0], "ag2", k)

    back = [None] * CHUNKS
    for o in range(1, nc):
        j = cpeer(o)
        arrived(place0(st, j), at["s0"] + j)

    def target_cols(plane_half):
        return pl.ds(pl.multiple_of((2 * plane_half + q) * df, df), df)

    send(
        tg.at[:, :, p, :, target_cols(1 - b)], tgp.at[b], at["tg"], (far, c)
    )
    tgp[b] = tg[:, :, p, :, target_cols(b)]
    run = dict(
        into_hidden=into_hidden, hidden=hidden, other_terms=other_terms, next_state=next_state,
        last_grad=last_grad, into_back=into_back, hidden_grad=hidden_grad, first_grad=first_grad,
    )
    for name, u, k in stage_order():
        if name == "next_state" and u == 0 and k == 0:
            arrived(tgp.at[1 - b], at["tg"])
        run[name](u, k)

    def out(acc, u, left, right, first):
        val = mm(left, right, over_rows)
        acc[...] = val if first else acc[...] + val

    def near_out(acc, u, left, right, first):
        out(acc, u, flat(left[u]), flat(right[u]), first)

    from_near("h", hb, 1)
    from_near("g", gb, 1)
    out(gwo, 1, flat(hf[1]), flat(gf[1, :, a]), True)
    near_out(gwo, 1, hb, gb, False)
    from_near("s", sb, 1)
    from_near("e", eb, 1)
    out(gwi, 1, flat(sf[1, :, a]), flat(ef[1]), True)
    near_out(gwi, 1, sb, eb, False)
    from_near("h", hb, 0)
    from_near("g", gb, 0)
    out(gwo, 0, flat(hf[0]), flat(gf[0, :, a]), False)
    near_out(gwo, 0, hb, gb, False)
    from_near("s", sb, 0)
    out(gwi, 0, flat(sf[0, :, a]), flat(ef[0]), False)
    from_near("e", eb, 0)
    near_out(gwi, 0, sb, eb, False)

    for src, dst, sem, slot, dev, when in started:
        if when is None:
            copy(src, dst, sem, slot, dev).wait_send()
        else:
            pl.when(when)(lambda: copy(src, dst, sem, slot, dev).wait_send())


def paired(nc, state_start, actions, targets, w_in, w_out, action_embed):
    rb, sw = state_start.shape
    df, fc = w_in.shape
    groups = nc // 2
    per = CHUNKS // 2
    piece = rb // (per * groups)
    rows = groups * piece
    vm = pl.BlockSpec(memory_space=pltpu.VMEM)
    _, receives = sem_plan(nc)
    state = pltpu.VMEM((2, CHUNKS, 2, groups, piece, df), BF16)
    hid = pltpu.VMEM((2, CHUNKS, rows, fc), BF16)
    feat = pltpu.VMEM((2, CHUNKS, rows, df), BF16)
    return pl.pallas_call(
        kernel,
        out_shape=(
            jax.ShapeDtypeStruct((df, fc), F32),
            jax.ShapeDtypeStruct((fc, df), F32),
        ),
        in_specs=[vm] * 6,
        out_specs=(vm, vm),
        scratch_shapes=[
            pltpu.VMEM((df, fc), BF16),
            pltpu.VMEM((fc, df), BF16),
            pltpu.VMEM((per, groups, piece, sw), BF16),
            pltpu.VMEM((2, 2, per, piece, df), BF16),
            state,
            state,
            hid,
            hid,
            pltpu.VMEM((2, CHUNKS, groups, piece, df), BF16),
            pltpu.VMEM((2, CHUNKS, groups, piece, df), BF16),
            hid,
            hid,
            pltpu.VMEM((4, CHUNKS, rows, fc), BF16),
            pltpu.VMEM((4, CHUNKS, rows, fc), BF16),
            pltpu.VMEM((3, CHUNKS, 2, groups, piece, df), BF16),
            pltpu.VMEM((3, CHUNKS, nc, piece, df), BF16),
            pltpu.VMEM((2, CHUNKS, piece, df), BF16),
            pltpu.VMEM((2, CHUNKS, rows, fc), F32),
            pltpu.VMEM((2, CHUNKS, piece, 128), F32),
            pltpu.VMEM((2, CHUNKS, 4, piece, 128), F32),
            pltpu.SemaphoreType.DMA((sends_in_all(nc),)),
            pltpu.SemaphoreType.DMA((receives,)),
        ],
        compiler_params=pltpu.CompilerParams(
            collective_id=0, has_side_effects=True, vmem_limit_bytes=56 * 1024 * 1024
        ),
    )(
        state_start.reshape(per, groups, piece, sw),
        actions,
        targets.reshape(targets.shape[0], per, groups, piece, targets.shape[2]),
        w_in,
        w_out,
        action_embed,
    )


def solution(mesh):
    nr, nc = mesh.shape["row"], mesh.shape["col"]

    def on_device(state_start, actions, targets, w_in, w_out, action_embed):
        rb, sw = state_start.shape
        fits = (
            targets.shape[0] == 2
            and nr == 4
            and nc == 8
            and rb % (16 * (CHUNKS // 2) * (nc // 2)) == 0
            and sw % 128 == 0
            and w_in.shape[0] == 2 * sw
            and w_in.shape[1] % (128 * CHUNKS) == 0
        )
        args = (state_start, actions, targets, w_in, w_out, action_embed)
        if fits:
            return paired(nc, *args)
        return gathered(*args)

    in_specs = (
        P("row", "col"),
        P("row", None),
        P(None, "row", None),
        P("row", "col"),
        P("col", "row"),
        P(None, "col"),
    )
    out_specs = (P("row", "col"), P("col", "row"))
    return jax.shard_map(
        on_device, mesh=mesh, in_specs=in_specs, out_specs=out_specs, check_vma=False
    )
```

time: 147 us -> 122 us (0.83); the launches traced: 145 us -> 122 us
  Pallas kernels: 139 us -> 116 us
    pallas_call x1, Pallas kernels: 139 us -> 116 us  [paired(): pl.pallas_call(kernel, out_shape=(jax.ShapeDtypeStruct((df, fc), F32), ja...]
where the time goes in v1:
time: 122 us
  Pallas kernels  116 us (95%)
  local copies, waits for them, and re-layouts  4.74 us (4%)
    pallas_call x1, Pallas kernels, paired(): pl.pallas_call(kernel, out_shape=(jax.ShapeDtypeStruct((df, fc), F32), ja...  116 us
    unnamed x7, local copies, waits for them, and re-layouts  4.74 us

profile of v1, /device:TPU:0, one launch (start us, length us, event | category | flops | bytes accessed | tf_op | source)
XLA Modules:
  0.0 121.9 jit_solution(5840783260196565704)
XLA Ops:
  0.6 0.0 copy-start.1
  0.6 0.7 copy-done.1
  1.3 0.7 copy.8.act
  2.0 116.5 %shard_map.77 = (f32[512,512]{1,0:T(8,128)}, f32[512,512]{1,0:T(8,128)}) custom-call(bf16[2,4,16,256]{3,2,1,0:T(8,128)(2,1)} %bitcast.3, s32[128,2]{1,0:T(8,128)} %copy.8.act, bf16[2,2,4,16,2048]{4,3,2,1,0:T(8,128)(2,1)} %bitcast.2, bf16[512,512]{1,0:T(8,128)(2,1)} %wi.1, bf16[512,512]{1,0:T(8,128)(2,1)} %wo.1, bf16[18,512]{1,0:T(8,128)(2,1)} %emb.1), custom_call_target="tpu_custom_call" | custom-call | tf_op jit(solution)/shard_map/pallas_call | solution.py:463
  118.6 0.0 copy-start
  118.6 2.4 %copy.11 = f32[512,512]{1,0:T(8,128)} copy(f32[512,512]{1,0:T(8,128)} %get-tuple-element.4) | data formatting | bytes 2097152
  120.9 0.0 copy-done
  120.9 1.0 copy.12
Async XLA Ops:
  0.6 0.7 copy-start.1
  118.6 2.4 %copy-start = (f32[512,512]{1,0:T(8,128)S(1)}, f32[512,512]{1,0:T(8,128)}, u32[]{:S(2)}) copy-start(f32[512,512]{1,0:T(8,128)} %get-tuple-element.5) | copy-start | bytes 3145732

commit v2 on v1

--- a/solution.py
+++ b/solution.py
@@ -147,6 +147,7 @@
     total = 0
     for name, count in (
         [("wi", 1), ("wo", CHUNKS), ("s0x", 1), ("s0", nc), ("tg", 1)]
+        + [(f"{n}t{u}", CHUNKS) for n in "sg" for u in range(2)]
         + [(f"ag{i}", CHUNKS * nc) for i in range(3)]
         + [(f"z{i}", CHUNKS) for i in range(4)]
         + [(f"rs{i}", CHUNKS * nc) for i in range(3)]
@@ -159,13 +160,13 @@
 
 
 def sends_in_all(nc):
-    return 3 + CHUNKS + 2 * (nc - 1) + CHUNKS * (6 * (nc - 1) + 3 + 4 + 6 + 8)
+    return 3 + CHUNKS + 2 * nc + CHUNKS * (6 * (nc - 1) + 3 + 4 + 6 + 8 + 4)
 
 
 def kernel(
-    st, act, tg, wi, wo, emb, gwi, gwo,
-    wix, wox, s0x, tgp, sf, gf, hf, ef, sb, gb, hb, eb, zs, zr, ys, cr, own, pre, ds, dz,
-    send_sem, recv_sem,
+    st, act_in, tg, wi_in, wo_in, emb_in, gwi_out, gwo_out,
+    wi, wo, act, emb, gwi, gwo, wix, wox, s0x, tgp, sf, gf, hf, ef, sb, gb, hb, eb, zs, zr, ys, cr, own, pre, ds, dz,
+    send_sem, recv_sem, load_sem,
 ):
     r, c = lax.axis_index("row"), lax.axis_index("col")
     nr, nc = 4, 8
@@ -204,6 +205,33 @@
         else:
             pl.when(when)(lambda: copy(dst, dst, 0, slot, (near, c)).wait_recv())
 
+    home = lax.div(c, nc // 2) == b
+    away = jnp.logical_not(home)
+
+    def place0(col):
+        i = jnp.where(lax.div(col, nc // 2) == b, b, 1 - b)
+        return sf.at[
+            0, pl.ds(i * per, per), lax.rem(lax.div(col, 2), 2), :, :,
+            pl.ds(pl.multiple_of(lax.rem(col, 2) * sw, sw), sw),
+        ]
+
+    def target_cols(plane_half):
+        return pl.ds(pl.multiple_of((2 * plane_half + q) * df, df), df)
+
+    loads = [
+        pltpu.make_async_copy(src, dst, load_sem.at[i])
+        for i, (src, dst) in enumerate((
+            (wi_in, wi), (act_in, act), (emb_in, emb), (wo_in, wo),
+            (tg.at[:, :, p, :, target_cols(b)], tgp.at[b]),
+        ))
+    ]
+    keep = pltpu.make_async_copy(st, place0(c), load_sem.at[5])
+    for load in loads:
+        load.start()
+    pl.when(home)(lambda: keep.start())
+    gwo_store = pltpu.make_async_copy(gwo, gwo_out, load_sem.at[6])
+    gwi_store = pltpu.make_async_copy(gwi, gwi_out, load_sem.at[7])
+
     barrier = pltpu.get_barrier_semaphore()
     greeted = [(r, cpeer(o)) for o in range(1, nc)] + [
         (near, c), (far, c), (far, twin), (far, cpeer(nc // 2))
@@ -212,37 +240,31 @@
         pl.semaphore_signal(barrier, inc=1, device_id=dev, device_id_type=MESH)
     pl.semaphore_wait(barrier, len(greeted))
 
-    home = lax.div(c, nc // 2) == b
-    away = jnp.logical_not(home)
     send(st, s0x, at["s0x"], (far, cpeer(nc // 2)), away)
-    send(wi, wix, at["wi"], (near, c))
-
-    def place0(block, col):
-        i = jnp.where(lax.div(col, nc // 2) == b, b, 1 - b)
-        return sf.at[
-            0, pl.ds(i * per, per), lax.rem(lax.div(col, 2), 2), :, :,
-            pl.ds(pl.multiple_of(lax.rem(col, 2) * sw, sw), sw),
-        ]
-
-    for o in range(1, nc):
-        send(st, place0(st, c), at["s0"] + c, (r, cpeer(o)), home)
+    for o in (nc // 2, 2, nc - 2):
+        send(st, place0(c), at["s0"] + c, (r, cpeer(o)), home)
+    send(st, place0(c), at["s0"] + c, (r, twin), home)
+    send(wi_in, wix, at["wi"], (near, c))
+
+    def send_wo(j):
+        part = pl.ds(j * (wo.shape[0] // CHUNKS), wo.shape[0] // CHUNKS)
+        send(wo_in.at[part], wox.at[part], at["wo"] + j, (near, c))
+
+    send_wo(0)
     arrived(s0x, at["s0x"], away)
-    for o in range(1, nc):
-        send(s0x, place0(s0x, c), at["s0"] + c, (r, cpeer(o)), away)
-
-    @pl.when(home)
-    def _():
-        place0(st, c)[...] = st[...]
+    for o in (nc // 2, 2, nc - 2):
+        send(s0x, place0(c), at["s0"] + c, (r, cpeer(o)), away)
+    send(s0x, place0(c), at["s0"] + c, (r, twin), away)
 
     @pl.when(away)
     def _():
-        place0(s0x, c)[...] = s0x[...]
-
-    def send_wo(j):
-        part = pl.ds(j * (wo.shape[0] // CHUNKS), wo.shape[0] // CHUNKS)
-        send(wo.at[part], wox.at[part], at["wo"] + j, (near, c))
-
-    send_wo(0)
+        place0(c)[...] = s0x[...]
+
+    for o in (nc // 2, 2, nc - 2):
+        j = cpeer(o)
+        arrived(place0(j), at["s0"] + j)
+        send(place0(j), place0(j), at["s0"] + j, (r, twin))
+    pl.when(home)(lambda: keep.wait())
 
     def mm(x, y, dims):
         return lax.dot_general(x, y, (dims, ((), ())), preferred_element_type=F32)
@@ -250,7 +272,7 @@
     def flat(x):
         return x.reshape(-1, x.shape[-1])
 
-    ids = lax.broadcasted_iota(jnp.int32, (rows, emb.shape[0]), 1)
+    ids = lax.broadcasted_iota(jnp.int32, (emb.shape[0], per * rows), 0)
     plain, flipped, over_rows = ((1,), (0,)), ((1,), (1,)), ((0,), (0,))
 
     def spread(full, name, k):
@@ -272,6 +294,20 @@
 
     def to_near(name, u, k, src, dst):
         send(src, dst.at[u, k], at[f"{name}b{u}"] + k, (near, c))
+
+    mine = pl.ds(q * (groups // 2), groups // 2)
+    others = pl.ds((1 - q) * (groups // 2), groups // 2)
+
+    def half_to_near(name, u, k, src, dst):
+        send(src.at[u, k, 1 - a, mine], dst.at[u, k, mine], at[f"{name}b{u}"] + k, (near, c))
+
+    def half_to_twin(name, u, k, dst):
+        arrived(dst.at[u, k, mine], at[f"{name}b{u}"] + k)
+        send(dst.at[u, k, mine], dst.at[u, k, mine], at[f"{name}t{u}"] + k, (r, twin))
+
+    def from_twin(name, dst, u):
+        for k in range(CHUNKS):
+            arrived(dst.at[u, k, others], at[f"{name}t{u}"] + k)
 
     def from_near(name, dst, u):
         for k in range(CHUNKS):
@@ -332,15 +368,17 @@
         if u == 0 and k == 0:
             arrived(wix, at["wi"])
         part = part + mm(flat(sf[u, k, 1 - a]), wix[...], plain)
-        act_k = act[rows * (k % per):rows * (k % per) + rows, u:u + 1]
-        mine = jnp.where(k // per == b, 0, -emb.shape[0])
-        onehot = (act_k + mine == ids).astype(F32).astype(BF16)
-        part = part + mm(onehot, emb[...], plain)
+        part = part + acts[u][rows * (k % per):rows * (k % per) + rows] * jnp.where(k // per == b, 1.0, 0.0)
         pre[u, k] = part
         exchange(u, k, part)
         if u == 0 and k < CHUNKS - 1:
             send_wo(k + 1)
-        to_near("s", u, k, sf.at[u, k, 1 - a], sb)
+        if u == 0 and k == CHUNKS - 1:
+            send(
+                tg.at[:, :, p, :, target_cols(1 - b)], tgp.at[b], at["tg"], (far, c)
+            )
+        if u == 1:
+            to_near("h", 0, k, hf.at[0, k], hb)
 
     def hidden(u, k):
         v = pre[u, k] + exchanged(u, k)
@@ -357,7 +395,8 @@
                 part = pl.ds(j * (wo.shape[0] // CHUNKS), wo.shape[0] // CHUNKS)
                 arrived(wox.at[part], at["wo"] + j)
         terms(u, k, hf[u, k], wox, plain, 1 - a)
-        to_near("h", u, k, hf.at[u, k], hb)
+        if u == 1:
+            to_near("h", 1, k, hf.at[1, k], hb)
 
     def next_state(u, k):
         new = (sf[u, k, q, p].astype(F32) + total(u, k)).astype(BF16)
@@ -379,7 +418,11 @@
         )
         back[k] = part
         exchange(3 - u, k, part)
-        to_near("g", u, k, gf.at[u, k, 1 - a], gb)
+        for v in range(2):
+            if u == 1:
+                half_to_near("s", v, k, sf, sb)
+            else:
+                half_to_near("g", v, k, gf, gb)
 
     def hidden_grad(u, k):
         ef[u, k] = ((back[k] + exchanged(3 - u, k)) * pre[u, k]).astype(BF16)
@@ -389,6 +432,8 @@
         to_near("e", u, k, ef.at[u, k], eb)
 
     def first_grad(u, k):
+        for v in range(2):
+            half_to_twin("s", v, k, sb)
         if k == 0:
             for j in range(CHUNKS):
                 dots_in(0, j)
@@ -397,17 +442,16 @@
         spread(gf.at[0], "ag2", k)
 
     back = [None] * CHUNKS
-    for o in range(1, nc):
+    for o in (nc // 2, 2, nc - 2):
         j = cpeer(o)
-        arrived(place0(st, j), at["s0"] + j)
-
-    def target_cols(plane_half):
-        return pl.ds(pl.multiple_of((2 * plane_half + q) * df, df), df)
-
-    send(
-        tg.at[:, :, p, :, target_cols(1 - b)], tgp.at[b], at["tg"], (far, c)
-    )
-    tgp[b] = tg[:, :, p, :, target_cols(b)]
+        j = j + 1 - 2 * q
+        arrived(place0(j), at["s0"] + j)
+    arrived(place0(twin), at["s0"] + twin)
+    for load in loads[:3]:
+        load.wait()
+    acts = [
+        mm((act[u:u + 1] == ids).astype(F32).astype(BF16), emb[...], over_rows) for u in range(2)
+    ]
     run = dict(
         into_hidden=into_hidden, hidden=hidden, other_terms=other_terms, next_state=next_state,
         last_grad=last_grad, into_back=into_back, hidden_grad=hidden_grad, first_grad=first_grad,
@@ -415,6 +459,9 @@
     for name, u, k in stage_order():
         if name == "next_state" and u == 0 and k == 0:
             arrived(tgp.at[1 - b], at["tg"])
+            loads[4].wait()
+        if name == "hidden" and u == 0 and k == 0:
+            loads[3].wait()
         run[name](u, k)
 
     def out(acc, u, left, right, first):
@@ -424,28 +471,35 @@
     def near_out(acc, u, left, right, first):
         out(acc, u, flat(left[u]), flat(right[u]), first)
 
+    for u in range(2):
+        for k in range(CHUNKS):
+            half_to_twin("g", u, k, gb)
     from_near("h", hb, 1)
-    from_near("g", gb, 1)
+    from_near("h", hb, 0)
     out(gwo, 1, flat(hf[1]), flat(gf[1, :, a]), True)
+    out(gwo, 0, flat(hf[0]), flat(gf[0, :, a]), False)
+    from_twin("g", gb, 1)
+    from_twin("g", gb, 0)
     near_out(gwo, 1, hb, gb, False)
-    from_near("s", sb, 1)
+    near_out(gwo, 0, hb, gb, False)
+    gwo_store.start()
+    from_twin("s", sb, 1)
+    from_twin("s", sb, 0)
     from_near("e", eb, 1)
     out(gwi, 1, flat(sf[1, :, a]), flat(ef[1]), True)
+    out(gwi, 0, flat(sf[0, :, a]), flat(ef[0]), False)
     near_out(gwi, 1, sb, eb, False)
-    from_near("h", hb, 0)
-    from_near("g", gb, 0)
-    out(gwo, 0, flat(hf[0]), flat(gf[0, :, a]), False)
-    near_out(gwo, 0, hb, gb, False)
-    from_near("s", sb, 0)
-    out(gwi, 0, flat(sf[0, :, a]), flat(ef[0]), False)
-    from_near("e", eb, 0)
-    near_out(gwi, 0, sb, eb, False)
 
     for src, dst, sem, slot, dev, when in started:
         if when is None:
             copy(src, dst, sem, slot, dev).wait_send()
         else:
             pl.when(when)(lambda: copy(src, dst, sem, slot, dev).wait_send())
+    from_near("e", eb, 0)
+    near_out(gwi, 0, sb, eb, False)
+    gwi_store.start()
+    gwo_store.wait()
+    gwi_store.wait()
 
 
 def paired(nc, state_start, actions, targets, w_in, w_out, action_embed):
@@ -455,7 +509,7 @@
     per = CHUNKS // 2
     piece = rb // (per * groups)
     rows = groups * piece
-    vm = pl.BlockSpec(memory_space=pltpu.VMEM)
+    hbm = pl.BlockSpec(memory_space=pltpu.HBM)
     _, receives = sem_plan(nc)
     state = pltpu.VMEM((2, CHUNKS, 2, groups, piece, df), BF16)
     hid = pltpu.VMEM((2, CHUNKS, rows, fc), BF16)
@@ -466,9 +520,15 @@
             jax.ShapeDtypeStruct((df, fc), F32),
             jax.ShapeDtypeStruct((fc, df), F32),
         ),
-        in_specs=[vm] * 6,
-        out_specs=(vm, vm),
+        in_specs=[hbm] * 6,
+        out_specs=(hbm, hbm),
         scratch_shapes=[
+            pltpu.VMEM((df, fc), BF16),
+            pltpu.VMEM((fc, df), BF16),
+            pltpu.VMEM((2, rb), jnp.int32),
+            pltpu.VMEM(action_embed.shape, BF16),
+            pltpu.VMEM((df, fc), F32),
+            pltpu.VMEM((fc, df), F32),
             pltpu.VMEM((df, fc), BF16),
             pltpu.VMEM((fc, df), BF16),
             pltpu.VMEM((per, groups, piece, sw), BF16),
@@ -491,13 +551,14 @@
             pltpu.VMEM((2, CHUNKS, 4, piece, 128), F32),
             pltpu.SemaphoreType.DMA((sends_in_all(nc),)),
             pltpu.SemaphoreType.DMA((receives,)),
+            pltpu.SemaphoreType.DMA((8,)),
         ],
         compiler_params=pltpu.CompilerParams(
             collective_id=0, has_side_effects=True, vmem_limit_bytes=56 * 1024 * 1024
         ),
     )(
         state_start.reshape(per, groups, piece, sw),
-        actions,
+        actions.T,
         targets.reshape(targets.shape[0], per, groups, piece, targets.shape[2]),
         w_in,
         w_out,

time: 122 us -> 115 us (0.943)
  Pallas kernels: 116 us -> 111 us
  local copies, waits for them, and re-layouts: 4.74 us -> 3.32 us
    pallas_call x1, Pallas kernels: 116 us -> 111 us  [paired(): pl.pallas_call(kernel, out_shape=(jax.ShapeDtypeStruct((df, fc), F32), ja...]
    unnamed x7 -> x4, local copies, waits for them, and re-layouts: 4.74 us -> 3.32 us
where the time goes in v2:
time: 115 us
  Pallas kernels  111 us (97%)
  local copies, waits for them, and re-layouts  3.32 us (3%)
    pallas_call x1, Pallas kernels, paired(): pl.pallas_call(kernel, out_shape=(jax.ShapeDtypeStruct((df, fc), F32), ja...  111 us
    unnamed x4, local copies, waits for them, and re-layouts  3.32 us

profile of v2, /device:TPU:0, one launch (start us, length us, event | category | flops | bytes accessed | tf_op | source)
XLA Modules:
  0.0 114.9 jit_solution(16813212125524933829)
XLA Ops:
  0.6 110.9 %shard_map.77 = (f32[512,512]{1,0:T(8,128)}, f32[512,512]{1,0:T(8,128)}) custom-call(bf16[2,4,16,256]{3,2,1,0:T(8,128)(2,1)} %bitcast.4, s32[2,128]{1,0:T(2,128)} %bitcast.5, bf16[2,2,4,16,2048]{4,3,2,1,0:T(8,128)(2,1)} %bitcast.3, bf16[512,512]{1,0:T(8,128)(2,1)} %wi_in.1, bf16[512,512]{1,0:T(8,128)(2,1)} %wo_in.1, bf16[18,512]{1,0:T(8,128)(2,1)} %emb_in.1), custom_call_target="tpu_custom_call" | custom-call | tf_op jit(solution)/shard_map/pallas_call | solution.py:517
  111.6 0.0 copy-start
  111.6 2.4 %copy.10 = f32[512,512]{1,0:T(8,128)} copy(f32[512,512]{1,0:T(8,128)} %get-tuple-element.4) | data formatting | bytes 2097152
  113.9 0.0 copy-done
  113.9 1.0 copy.11
Async XLA Ops:
  111.6 2.4 %copy-start = (f32[512,512]{1,0:T(8,128)S(1)}, f32[512,512]{1,0:T(8,128)}, u32[]{:S(2)}) copy-start(f32[512,512]{1,0:T(8,128)} %get-tuple-element.5) | copy-start | bytes 3145732

commit v3 on v2

--- a/solution.py
+++ b/solution.py
@@ -148,6 +148,7 @@
     for name, count in (
         [("wi", 1), ("wo", CHUNKS), ("s0x", 1), ("s0", nc), ("tg", 1)]
         + [(f"{n}t{u}", CHUNKS) for n in "sg" for u in range(2)]
+        + [(f"{n}p{u}", 4) for n in "sg" for u in range(2)]
         + [(f"ag{i}", CHUNKS * nc) for i in range(3)]
         + [(f"z{i}", CHUNKS) for i in range(4)]
         + [(f"rs{i}", CHUNKS * nc) for i in range(3)]
@@ -160,7 +161,7 @@
 
 
 def sends_in_all(nc):
-    return 3 + CHUNKS + 2 * nc + CHUNKS * (6 * (nc - 1) + 3 + 4 + 6 + 8 + 4)
+    return 3 + CHUNKS + 2 * nc + CHUNKS * (6 * (nc - 1) + 3 + 4 + 6 + 8 + 4) + 12
 
 
 def kernel(
@@ -182,8 +183,14 @@
     started = []
     unused = iter(range(10000))
 
+    def toggled(v, bits):
+        for bit in (1, 2, 4):
+            if bits & bit:
+                v = v + bit - 2 * bit * lax.rem(lax.div(v, bit), 2)
+        return v
+
     def cpeer(o):
-        return lax.rem(c + o, nc)
+        return toggled(c, (6, 7, 4, 5, 2, 3, 1)[o - 1])
 
     def copy(src, dst, sem, slot, dev):
         return pltpu.make_async_remote_copy(
@@ -234,15 +241,15 @@
 
     barrier = pltpu.get_barrier_semaphore()
     greeted = [(r, cpeer(o)) for o in range(1, nc)] + [
-        (near, c), (far, c), (far, twin), (far, cpeer(nc // 2))
+        (near, c), (far, c), (far, twin), (far, toggled(c, 4))
     ]
     for dev in greeted:
         pl.semaphore_signal(barrier, inc=1, device_id=dev, device_id_type=MESH)
     pl.semaphore_wait(barrier, len(greeted))
 
-    send(st, s0x, at["s0x"], (far, cpeer(nc // 2)), away)
-    for o in (nc // 2, 2, nc - 2):
-        send(st, place0(c), at["s0"] + c, (r, cpeer(o)), home)
+    send(st, s0x, at["s0x"], (far, toggled(c, 4)), away)
+    for o in (6, 4, 2):
+        send(st, place0(c), at["s0"] + c, (r, toggled(c, o)), home)
     send(st, place0(c), at["s0"] + c, (r, twin), home)
     send(wi_in, wix, at["wi"], (near, c))
 
@@ -252,16 +259,16 @@
 
     send_wo(0)
     arrived(s0x, at["s0x"], away)
-    for o in (nc // 2, 2, nc - 2):
-        send(s0x, place0(c), at["s0"] + c, (r, cpeer(o)), away)
+    for o in (6, 4, 2):
+        send(s0x, place0(c), at["s0"] + c, (r, toggled(c, o)), away)
     send(s0x, place0(c), at["s0"] + c, (r, twin), away)
 
     @pl.when(away)
     def _():
         place0(c)[...] = s0x[...]
 
-    for o in (nc // 2, 2, nc - 2):
-        j = cpeer(o)
+    for o in (4, 2, 6):
+        j = toggled(c, o)
         arrived(place0(j), at["s0"] + j)
         send(place0(j), place0(j), at["s0"] + j, (r, twin))
     pl.when(home)(lambda: keep.wait())
@@ -305,6 +312,24 @@
         arrived(dst.at[u, k, mine], at[f"{name}b{u}"] + k)
         send(dst.at[u, k, mine], dst.at[u, k, mine], at[f"{name}t{u}"] + k, (r, twin))
 
+    def piece_to_near(name, u, k, src, dst):
+        send(src.at[k, q, p], dst.at[u, k, p], at[f"{name}b{u}"] + k, (near, c), q != a)
+
+    def share(name, u, dst):
+        for k in range(CHUNKS):
+            arrived(dst.at[u, k, p], at[f"{name}b{u}"] + k, q == a)
+        for o in (6, 4, 2):
+            send(dst.at[u, :, p], dst.at[u, :, p], at[f"{name}p{u}"] + p, (r, toggled(c, o)), q == a)
+
+    def complete(name, u, dst):
+        for o in (1, 2, 3):
+            g = toggled(p, o)
+            arrived(dst.at[u, :, g], at[f"{name}p{u}"] + g, q == a)
+        send(dst.at[u], dst.at[u], at[f"{name}t{u}"], (r, twin), q == a)
+
+    def completed(name, u, dst):
+        arrived(dst.at[u], at[f"{name}t{u}"], q != a)
+
     def from_twin(name, dst, u):
         for k in range(CHUNKS):
             arrived(dst.at[u, k, others], at[f"{name}t{u}"] + k)
@@ -316,7 +341,7 @@
     def terms(phase, k, left, weight, dims, which):
         ys[phase, k, which] = mm(left, weight[...], dims).astype(BF16).reshape(groups, piece, df)
         for o in range(groups - 1, -1, -1):
-            g = lax.rem(p + o, groups)
+            g = toggled(p, o)
             send(
                 ys.at[phase, k, which, g], cr.at[phase, k, c], at[f"rs{phase}"] + k * nc + c,
                 (r, 2 * g + which), which != q if o == 0 else None,
@@ -404,12 +429,14 @@
         if u == 0:
             sf[1, k, q, p] = new
             spread(sf.at[1], "ag0", k)
+            piece_to_near("s", 1, k, sf.at[1], sb)
         dots(u, k)
 
     def last_grad(u, k):
         dots_in(u, k)
         gf[1, k, q, p] = cosine(u, k).astype(BF16)
         spread(gf.at[1], "ag1", k)
+        piece_to_near("g", 1, k, gf.at[1], gb)
 
     def into_back(u, k):
         collect(gf.at[u], f"ag{2 - u}", k)
@@ -418,11 +445,8 @@
         )
         back[k] = part
         exchange(3 - u, k, part)
-        for v in range(2):
-            if u == 1:
-                half_to_near("s", v, k, sf, sb)
-            else:
-                half_to_near("g", v, k, gf, gb)
+        if u == 1:
+            half_to_near("s", 0, k, sf, sb)
 
     def hidden_grad(u, k):
         ef[u, k] = ((back[k] + exchanged(3 - u, k)) * pre[u, k]).astype(BF16)
@@ -432,18 +456,18 @@
         to_near("e", u, k, ef.at[u, k], eb)
 
     def first_grad(u, k):
-        for v in range(2):
-            half_to_twin("s", v, k, sb)
+        half_to_twin("s", 0, k, sb)
         if k == 0:
             for j in range(CHUNKS):
                 dots_in(0, j)
         summed = gf[1, k, q, p].astype(F32) + total(2, k) + cosine(0, k)
         gf[0, k, q, p] = summed.astype(BF16)
         spread(gf.at[0], "ag2", k)
+        piece_to_near("g", 0, k, gf.at[0], gb)
 
     back = [None] * CHUNKS
-    for o in (nc // 2, 2, nc - 2):
-        j = cpeer(o)
+    for o in (4, 2, 6):
+        j = toggled(c, o)
         j = j + 1 - 2 * q
         arrived(place0(j), at["s0"] + j)
     arrived(place0(twin), at["s0"] + twin)
@@ -463,6 +487,15 @@
         if name == "hidden" and u == 0 and k == 0:
             loads[3].wait()
         run[name](u, k)
+        if k == CHUNKS - 1:
+            if name == "into_hidden" and u == 1:
+                share("s", 1, sb)
+            elif name == "into_back" and u == 1:
+                complete("s", 1, sb)
+                share("g", 1, gb)
+            elif name == "into_back" and u == 0:
+                complete("g", 1, gb)
+                share("g", 0, gb)
 
     def out(acc, u, left, right, first):
         val = mm(left, right, over_rows)
@@ -471,19 +504,17 @@
     def near_out(acc, u, left, right, first):
         out(acc, u, flat(left[u]), flat(right[u]), first)
 
-    for u in range(2):
-        for k in range(CHUNKS):
-            half_to_twin("g", u, k, gb)
+    complete("g", 0, gb)
     from_near("h", hb, 1)
     from_near("h", hb, 0)
     out(gwo, 1, flat(hf[1]), flat(gf[1, :, a]), True)
     out(gwo, 0, flat(hf[0]), flat(gf[0, :, a]), False)
-    from_twin("g", gb, 1)
-    from_twin("g", gb, 0)
+    completed("g", 1, gb)
+    completed("g", 0, gb)
     near_out(gwo, 1, hb, gb, False)
     near_out(gwo, 0, hb, gb, False)
     gwo_store.start()
-    from_twin("s", sb, 1)
+    completed("s", 1, sb)
     from_twin("s", sb, 0)
     from_near("e", eb, 1)
     out(gwi, 1, flat(sf[1, :, a]), flat(ef[1]), True)

time: 115 us -> 109 us (0.948)
  Pallas kernels: 111 us -> 105 us
    pallas_call x1, Pallas kernels: 111 us -> 105 us  [paired(): pl.pallas_call(kernel, out_shape=(jax.ShapeDtypeStruct((df, fc), F32), ja...]
where the time goes in v3:
time: 109 us
  Pallas kernels  105 us (96%)
  local copies, waits for them, and re-layouts  3.32 us (3%)
    pallas_call x1, Pallas kernels, paired(): pl.pallas_call(kernel, out_shape=(jax.ShapeDtypeStruct((df, fc), F32), ja...  105 us
    unnamed x4, local copies, waits for them, and re-layouts  3.32 us

profile of v3, /device:TPU:0, one launch (start us, length us, event | category | flops | bytes accessed | tf_op | source)
XLA Modules:
  0.0 108.8 jit_solution(10140533599739264563)
XLA Ops:
  0.6 104.9 %shard_map.77 = (f32[512,512]{1,0:T(8,128)}, f32[512,512]{1,0:T(8,128)}) custom-call(bf16[2,4,16,256]{3,2,1,0:T(8,128)(2,1)} %bitcast.4, s32[2,128]{1,0:T(2,128)} %bitcast.5, bf16[2,2,4,16,2048]{4,3,2,1,0:T(8,128)(2,1)} %bitcast.3, bf16[512,512]{1,0:T(8,128)(2,1)} %wi_in.1, bf16[512,512]{1,0:T(8,128)(2,1)} %wo_in.1, bf16[18,512]{1,0:T(8,128)(2,1)} %emb_in.1), custom_call_target="tpu_custom_call" | custom-call | tf_op jit(solution)/shard_map/pallas_call | solution.py:548
  105.5 0.0 copy-start
  105.5 2.4 %copy.10 = f32[512,512]{1,0:T(8,128)} copy(f32[512,512]{1,0:T(8,128)} %get-tuple-element.4) | data formatting | bytes 2097152
  107.9 0.0 copy-done
  107.9 1.0 copy.11
Async XLA Ops:
  105.5 2.4 %copy-start = (f32[512,512]{1,0:T(8,128)S(1)}, f32[512,512]{1,0:T(8,128)}, u32[]{:S(2)}) copy-start(f32[512,512]{1,0:T(8,128)} %get-tuple-element.5) | copy-start | bytes 3145732

commit v4 on v3

--- a/solution.py
+++ b/solution.py
@@ -402,8 +402,6 @@
             send(
                 tg.at[:, :, p, :, target_cols(1 - b)], tgp.at[b], at["tg"], (far, c)
             )
-        if u == 1:
-            to_near("h", 0, k, hf.at[0, k], hb)
 
     def hidden(u, k):
         v = pre[u, k] + exchanged(u, k)
@@ -420,8 +418,7 @@
                 part = pl.ds(j * (wo.shape[0] // CHUNKS), wo.shape[0] // CHUNKS)
                 arrived(wox.at[part], at["wo"] + j)
         terms(u, k, hf[u, k], wox, plain, 1 - a)
-        if u == 1:
-            to_near("h", 1, k, hf.at[1, k], hb)
+        to_near("h", u, k, hf.at[u, k], hb)
 
     def next_state(u, k):
         new = (sf[u, k, q, p].astype(F32) + total(u, k)).astype(BF16)

time: 109 us -> 108 us (level)
  Pallas kernels: 105 us -> 103 us
    pallas_call x1, Pallas kernels: 105 us -> 103 us  [paired(): pl.pallas_call(kernel, out_shape=(jax.ShapeDtypeStruct((df, fc), F32), ja...]
where the time goes in v4:
time: 108 us; the launch traced here: 107 us
  Pallas kernels  103 us (95%)
  local copies, waits for them, and re-layouts  3.32 us (3%)
    pallas_call x1, Pallas kernels, paired(): pl.pallas_call(kernel, out_shape=(jax.ShapeDtypeStruct((df, fc), F32), ja...  103 us
    unnamed x4, local copies, waits for them, and re-layouts  3.32 us

profile of v4, /device:TPU:0, one launch (start us, length us, event | category | flops | bytes accessed | tf_op | source)
XLA Modules:
  0.0 107.2 jit_solution(10424365169014582140)
XLA Ops:
  0.6 103.2 %shard_map.77 = (f32[512,512]{1,0:T(8,128)}, f32[512,512]{1,0:T(8,128)}) custom-call(bf16[2,4,16,256]{3,2,1,0:T(8,128)(2,1)} %bitcast.4, s32[2,128]{1,0:T(2,128)} %bitcast.5, bf16[2,2,4,16,2048]{4,3,2,1,0:T(8,128)(2,1)} %bitcast.3, bf16[512,512]{1,0:T(8,128)(2,1)} %wi_in.1, bf16[512,512]{1,0:T(8,128)(2,1)} %wo_in.1, bf16[18,512]{1,0:T(8,128)(2,1)} %emb_in.1), custom_call_target="tpu_custom_call" | custom-call | tf_op jit(solution)/shard_map/pallas_call | solution.py:545
  103.9 0.0 copy-start
  103.9 2.4 %copy.10 = f32[512,512]{1,0:T(8,128)} copy(f32[512,512]{1,0:T(8,128)} %get-tuple-element.4) | data formatting | bytes 2097152
  106.2 0.0 copy-done
  106.2 1.0 copy.11
Async XLA Ops:
  103.9 2.4 %copy-start = (f32[512,512]{1,0:T(8,128)S(1)}, f32[512,512]{1,0:T(8,128)}, u32[]{:S(2)}) copy-start(f32[512,512]{1,0:T(8,128)} %get-tuple-element.5) | copy-start | bytes 3145732

commit v5 on v4

--- a/solution.py
+++ b/solution.py
@@ -237,7 +237,13 @@
         load.start()
     pl.when(home)(lambda: keep.start())
     gwo_store = pltpu.make_async_copy(gwo, gwo_out, load_sem.at[6])
-    gwi_store = pltpu.make_async_copy(gwi, gwi_out, load_sem.at[7])
+    gwi_stores = [
+        pltpu.make_async_copy(
+            gwi.at[pl.ds(j * (df // 2), df // 2)], gwi_out.at[pl.ds(j * (df // 2), df // 2)],
+            load_sem.at[7 + j],
+        )
+        for j in range(2)
+    ]
 
     barrier = pltpu.get_barrier_semaphore()
     greeted = [(r, cpeer(o)) for o in range(1, nc)] + [
@@ -396,6 +402,8 @@
         part = part + acts[u][rows * (k % per):rows * (k % per) + rows] * jnp.where(k // per == b, 1.0, 0.0)
         pre[u, k] = part
         exchange(u, k, part)
+        if u == 1:
+            half_to_near("s", 0, k, sf, sb)
         if u == 0 and k < CHUNKS - 1:
             send_wo(k + 1)
         if u == 0 and k == CHUNKS - 1:
@@ -442,8 +450,6 @@
         )
         back[k] = part
         exchange(3 - u, k, part)
-        if u == 1:
-            half_to_near("s", 0, k, sf, sb)
 
     def hidden_grad(u, k):
         ef[u, k] = ((back[k] + exchanged(3 - u, k)) * pre[u, k]).astype(BF16)
@@ -523,11 +529,18 @@
             copy(src, dst, sem, slot, dev).wait_send()
         else:
             pl.when(when)(lambda: copy(src, dst, sem, slot, dev).wait_send())
-    from_near("e", eb, 0)
-    near_out(gwi, 0, sb, eb, False)
-    gwi_store.start()
+    for k in range(CHUNKS - 1):
+        arrived(eb.at[0, k], at["eb0"] + k)
+    out(gwi, 0, flat(sb[0, :CHUNKS - 1]), flat(eb[0, :CHUNKS - 1]), False)
+    arrived(eb.at[0, CHUNKS - 1], at["eb0"] + CHUNKS - 1)
+    last = flat(sb[0, CHUNKS - 1])
+    for j in range(2):
+        part = slice(j * (df // 2), (j + 1) * (df // 2))
+        gwi[part] += mm(last[:, part], eb[0, CHUNKS - 1], over_rows)
+        gwi_stores[j].start()
     gwo_store.wait()
-    gwi_store.wait()
+    for j in range(2):
+        gwi_stores[j].wait()
 
 
 def paired(nc, state_start, actions, targets, w_in, w_out, action_embed):
@@ -579,7 +592,7 @@
             pltpu.VMEM((2, CHUNKS, 4, piece, 128), F32),
             pltpu.SemaphoreType.DMA((sends_in_all(nc),)),
             pltpu.SemaphoreType.DMA((receives,)),
-            pltpu.SemaphoreType.DMA((8,)),
+            pltpu.SemaphoreType.DMA((9,)),
         ],
         compiler_params=pltpu.CompilerParams(
             collective_id=0, has_side_effects=True, vmem_limit_bytes=56 * 1024 * 1024

time: 108 us -> 108 us (level)
  no operation moved by 1% of the time
where the time goes in v5:
time: 108 us; the launch traced here: 107 us
  Pallas kernels  103 us (95%)
  local copies, waits for them, and re-layouts  3.32 us (3%)
    pallas_call x1, Pallas kernels, paired(): pl.pallas_call(kernel, out_shape=(jax.ShapeDtypeStruct((df, fc), F32), ja...  103 us
    unnamed x4, local copies, waits for them, and re-layouts  3.32 us

profile of v5, /device:TPU:0, one launch (start us, length us, event | category | flops | bytes accessed | tf_op | source)
XLA Modules:
  0.0 107.1 jit_solution(1046432035808044388)
XLA Ops:
  0.6 103.1 %shard_map.77 = (f32[512,512]{1,0:T(8,128)}, f32[512,512]{1,0:T(8,128)}) custom-call(bf16[2,4,16,256]{3,2,1,0:T(8,128)(2,1)} %bitcast.4, s32[2,128]{1,0:T(2,128)} %bitcast.5, bf16[2,2,4,16,2048]{4,3,2,1,0:T(8,128)(2,1)} %bitcast.3, bf16[512,512]{1,0:T(8,128)(2,1)} %wi_in.1, bf16[512,512]{1,0:T(8,128)(2,1)} %wo_in.1, bf16[18,512]{1,0:T(8,128)(2,1)} %emb_in.1), custom_call_target="tpu_custom_call" | custom-call | tf_op jit(solution)/shard_map/pallas_call | solution.py:558
  103.8 0.0 copy-start
  103.8 2.4 %copy.10 = f32[512,512]{1,0:T(8,128)} copy(f32[512,512]{1,0:T(8,128)} %get-tuple-element.4) | data formatting | bytes 2097152
  106.1 0.0 copy-done
  106.1 1.0 copy.11
Async XLA Ops:
  103.8 2.4 %copy-start = (f32[512,512]{1,0:T(8,128)S(1)}, f32[512,512]{1,0:T(8,128)}, u32[]{:S(2)}) copy-start(f32[512,512]{1,0:T(8,128)} %get-tuple-element.5) | copy-start | bytes 3145732

commit v6 on v5

--- a/solution.py
+++ b/solution.py
@@ -225,6 +225,12 @@
     def target_cols(plane_half):
         return pl.ds(pl.multiple_of((2 * plane_half + q) * df, df), df)
 
+    barrier = pltpu.get_barrier_semaphore()
+    greeted = [(r, cpeer(o)) for o in range(1, nc)] + [
+        (near, c), (far, c), (far, twin), (far, toggled(c, 4))
+    ]
+    for dev in greeted:
+        pl.semaphore_signal(barrier, inc=1, device_id=dev, device_id_type=MESH)
     loads = [
         pltpu.make_async_copy(src, dst, load_sem.at[i])
         for i, (src, dst) in enumerate((
@@ -245,12 +251,6 @@
         for j in range(2)
     ]
 
-    barrier = pltpu.get_barrier_semaphore()
-    greeted = [(r, cpeer(o)) for o in range(1, nc)] + [
-        (near, c), (far, c), (far, twin), (far, toggled(c, 4))
-    ]
-    for dev in greeted:
-        pl.semaphore_signal(barrier, inc=1, device_id=dev, device_id_type=MESH)
     pl.semaphore_wait(barrier, len(greeted))
 
     send(st, s0x, at["s0x"], (far, toggled(c, 4)), away)

time: 108 us -> 108 us (level)
  no operation moved by 1% of the time
where the time goes in v6:
time: 108 us; the launch traced here: 107 us
  Pallas kernels  103 us (95%)
  local copies, waits for them, and re-layouts  3.32 us (3%)
    pallas_call x1, Pallas kernels, paired(): pl.pallas_call(kernel, out_shape=(jax.ShapeDtypeStruct((df, fc), F32), ja...  103 us
    unnamed x4, local copies, waits for them, and re-layouts  3.32 us

profile of v6, /device:TPU:0, one launch (start us, length us, event | category | flops | bytes accessed | tf_op | source)
XLA Modules:
  0.0 107.2 jit_solution(6137833280265342433)
XLA Ops:
  0.6 103.2 %shard_map.77 = (f32[512,512]{1,0:T(8,128)}, f32[512,512]{1,0:T(8,128)}) custom-call(bf16[2,4,16,256]{3,2,1,0:T(8,128)(2,1)} %bitcast.4, s32[2,128]{1,0:T(2,128)} %bitcast.5, bf16[2,2,4,16,2048]{4,3,2,1,0:T(8,128)(2,1)} %bitcast.3, bf16[512,512]{1,0:T(8,128)(2,1)} %wi_in.1, bf16[512,512]{1,0:T(8,128)(2,1)} %wo_in.1, bf16[18,512]{1,0:T(8,128)(2,1)} %emb_in.1), custom_call_target="tpu_custom_call" | custom-call | tf_op jit(solution)/shard_map/pallas_call | solution.py:558
  103.9 0.0 copy-start
  103.9 2.4 %copy.10 = f32[512,512]{1,0:T(8,128)} copy(f32[512,512]{1,0:T(8,128)} %get-tuple-element.4) | data formatting | bytes 2097152
  106.2 0.0 copy-done
  106.3 1.0 copy.11
Async XLA Ops:
  103.9 2.4 %copy-start = (f32[512,512]{1,0:T(8,128)S(1)}, f32[512,512]{1,0:T(8,128)}, u32[]{:S(2)}) copy-start(f32[512,512]{1,0:T(8,128)} %get-tuple-element.5) | copy-start | bytes 3145732

commit v7 on v4

--- a/solution.py
+++ b/solution.py
@@ -396,6 +396,8 @@
         part = part + acts[u][rows * (k % per):rows * (k % per) + rows] * jnp.where(k // per == b, 1.0, 0.0)
         pre[u, k] = part
         exchange(u, k, part)
+        if u == 1:
+            half_to_near("s", 0, k, sf, sb)
         if u == 0 and k < CHUNKS - 1:
             send_wo(k + 1)
         if u == 0 and k == CHUNKS - 1:
@@ -442,8 +444,6 @@
         )
         back[k] = part
         exchange(3 - u, k, part)
-        if u == 1:
-            half_to_near("s", 0, k, sf, sb)
 
     def hidden_grad(u, k):
         ef[u, k] = ((back[k] + exchanged(3 - u, k)) * pre[u, k]).astype(BF16)

time: 108 us -> 107 us (level)
  no operation moved by 1% of the time
where the time goes in v7:
time: 107 us
  Pallas kernels  103 us (96%)
  local copies, waits for them, and re-layouts  3.32 us (3%)
    pallas_call x1, Pallas kernels, paired(): pl.pallas_call(kernel, out_shape=(jax.ShapeDtypeStruct((df, fc), F32), ja...  103 us
    unnamed x4, local copies, waits for them, and re-layouts  3.32 us

profile of v7, /device:TPU:0, one launch (start us, length us, event | category | flops | bytes accessed | tf_op | source)
XLA Modules:
  0.0 107.2 jit_solution(1380856444243829431)
XLA Ops:
  0.6 103.2 %shard_map.77 = (f32[512,512]{1,0:T(8,128)}, f32[512,512]{1,0:T(8,128)}) custom-call(bf16[2,4,16,256]{3,2,1,0:T(8,128)(2,1)} %bitcast.4, s32[2,128]{1,0:T(2,128)} %bitcast.5, bf16[2,2,4,16,2048]{4,3,2,1,0:T(8,128)(2,1)} %bitcast.3, bf16[512,512]{1,0:T(8,128)(2,1)} %wi_in.1, bf16[512,512]{1,0:T(8,128)(2,1)} %wo_in.1, bf16[18,512]{1,0:T(8,128)(2,1)} %emb_in.1), custom_call_target="tpu_custom_call" | custom-call | tf_op jit(solution)/shard_map/pallas_call | solution.py:545
  103.9 0.0 copy-start
  103.9 2.4 %copy.10 = f32[512,512]{1,0:T(8,128)} copy(f32[512,512]{1,0:T(8,128)} %get-tuple-element.4) | data formatting | bytes 2097152
  106.2 0.0 copy-done
  106.2 1.0 copy.11
Async XLA Ops:
  103.9 2.4 %copy-start = (f32[512,512]{1,0:T(8,128)S(1)}, f32[512,512]{1,0:T(8,128)}, u32[]{:S(2)}) copy-start(f32[512,512]{1,0:T(8,128)} %get-tuple-element.5) | copy-start | bytes 3145732
